TPU v7x, 256 devices: a whole 4x4x8 slice. The times are simulated.
256 devices in a mesh: node: 16 (over z_hi, y), slab: 16 (over x, z_lo, core).
Axes of the slice: x: 4, y: 4, z: 8 (z_hi: 4, z_lo: 2; z = z_hi * 2 + z_lo), core: 2. Of those that a mesh axis runs over, the one named last changes fastest.
Arguments:
- tensors: float32 [16, 128, 128, 128], P('node', 'slab'), may hold values from -0.375 to 0.375
- ops: float32 [8, 128, 128], replicated, as said below
- assign: int32 [16, 2], replicated, may hold values from 0 to 7
- parent: int32 [16], replicated, may hold values from 0 to 7, as said below
- env: float32 [128, 128], replicated, as said below
Outputs:
- gradient: float32 [16, 128, 128, 128], P('node', None, 'slab')
- energy: float32 [], replicated
Inputs may be any that keep to these rules, and one draw needn't show every extreme that they name: parent[0] = 0 and parent[1] = 0; for every level L from 2 to 4, each node of indices 2 ** (L - 1) to 2 ** L - 1 has its parent among indices 2 ** (L - 2) to 2 ** (L - 1) - 1, and each of those is the parent of exactly two of them. Every matrix ops[k] is symmetric. env is symmetric.
All inputs are finite; a program needn't handle non-finite values.
Results may differ from a plain program's by a relative error of at most 0.00012.
Values sent between devices are 32-bit elements; how exact they have to be, the bound alone decides.
A program may use at most 64 MiB of HBM per device.

v0:
```python
import jax
import jax.numpy as jnp
from jax import lax
from jax.sharding import PartitionSpec as P

LEVELS = 5
NODES = 16
HIGH = lax.Precision.HIGHEST


def links(parent):
    index = jnp.arange(NODES, dtype=jnp.int32)
    linked = (parent[None, :] == index[:, None]) & (index[None, :] >= 1)
    count = jnp.sum(linked.astype(jnp.int32), axis=1)
    left = jnp.min(jnp.where(linked, index[None, :], NODES), axis=1)
    right = jnp.max(jnp.where(linked, index[None, :], -1), axis=1)
    return (count, left, right)


def lookup(table, wanted):
    slots = jnp.arange(table.shape[0], dtype=jnp.int32)
    return jnp.sum(jnp.where(slots[None, :] == wanted[:, None], table[None, :], 0), axis=1)


def select_rows(onehot, stacked):
    return jnp.einsum("nm,mab->nab", onehot, stacked, precision=HIGH)


def per_device(tensors, ops, assign, parent, env):
    local_count = tensors.shape[0]
    width = tensors.shape[2]
    slab_rows = width // lax.axis_size("slab")
    node_ids = lax.axis_index("node") * local_count + jnp.arange(local_count, dtype=jnp.int32)
    slots = jnp.arange(NODES, dtype=jnp.int32)
    levels_all = jnp.zeros((NODES,), jnp.int32)
    for power in range(LEVELS - 1):
        levels_all = levels_all + (slots >= 2**power).astype(jnp.int32)
    my_level = lookup(levels_all, node_ids)
    count, left, right = links(parent)
    my_count = lookup(count, node_ids)
    my_left = lookup(left, node_ids)
    my_right = lookup(right, node_ids)
    table_ids = jnp.arange(ops.shape[0], dtype=jnp.int32)
    first_hot = (lookup(assign[:, 0], node_ids)[:, None] == table_ids[None, :]).astype(jnp.float32)
    second_hot = (lookup(assign[:, 1], node_ids)[:, None] == table_ids[None, :]).astype(jnp.float32)
    first_ops = jnp.einsum("nk,kab->nab", first_hot, ops, precision=HIGH)
    second_ops = jnp.einsum("nk,kab->nab", second_hot, ops, precision=HIGH)
    pair = jnp.einsum("nplr,nlm->npmr", tensors, first_ops, precision=HIGH)
    pair = jnp.einsum("npmr,nrs->npms", pair, second_ops, precision=HIGH)
    right_form = lax.all_to_all(
        tensors.transpose(0, 3, 1, 2), "slab", split_axis=1, concat_axis=2, tiled=True
    )
    left_form, pair_left = (
        lax.all_to_all(tensors, "slab", split_axis=2, concat_axis=1, tiled=True),
        lax.all_to_all(pair, "slab", split_axis=2, concat_axis=1, tiled=True),
    )
    zero_square = jnp.zeros((width, width), jnp.float32)
    left_store = jnp.zeros_like(right_form)
    right_store = jnp.zeros_like(left_form)
    left_ops = first_ops
    right_ops = second_ops
    onehot_left = (my_left[:, None] == slots[None, :]).astype(jnp.float32)
    onehot_right = (my_right[:, None] == slots[None, :]).astype(jnp.float32)
    energy = jnp.zeros((), jnp.float32)
    for level in range(LEVELS - 1, -1, -1):

        def climb(items, level=level):
            right_part, left_part, pair_part, left_op, right_op, left_old, right_old, node_level = (
                items
            )

            def climb_compute(unused):
                along_left = jnp.einsum("rpl,lm->rpm", right_part, left_op, precision=HIGH)
                along_right = (
                    jnp.einsum("plr,rs->pls", left_part, right_op, precision=HIGH) + pair_part
                )
                upper = jnp.einsum("rpm,rqm->pq", along_left, right_part, precision=HIGH)
                upper = upper + jnp.einsum("pls,qls->pq", along_right, left_part, precision=HIGH)
                return (along_left, along_right, upper)

            def climb_keep(unused):
                return (left_old, right_old, zero_square)

            return lax.cond(node_level == level, climb_compute, climb_keep, 0)

        left_store, right_store, partial_up = lax.map(
            climb,
            (
                right_form,
                left_form,
                pair_left,
                left_ops,
                right_ops,
                left_store,
                right_store,
                my_level,
            ),
        )
        up_rows = lax.psum_scatter(partial_up, "slab", scatter_dimension=1, tiled=True)
        if level > 0:
            every_rows = lax.all_gather(up_rows, "node", axis=0, tiled=True)
            left_rows = select_rows(onehot_left, every_rows)
            right_rows = select_rows(onehot_right, every_rows)
            left_full, right_full = (
                lax.all_gather(left_rows, "slab", axis=1, tiled=True),
                lax.all_gather(right_rows, "slab", axis=1, tiled=True),
            )
            ready = my_level == level - 1
            left_ops = jnp.where((ready & (my_count >= 1))[:, None, None], left_full, left_ops)
            right_ops = jnp.where((ready & (my_count >= 2))[:, None, None], right_full, right_ops)
        else:
            env_rows = lax.dynamic_slice_in_dim(
                env, lax.axis_index("slab") * slab_rows, slab_rows, 0
            )
            own = jnp.where(node_ids == 0, jnp.sum(up_rows * env_rows[None], axis=(1, 2)), 0.0)
            energy = lax.psum(jnp.sum(own), ("node", "slab"))
    down = jnp.where((node_ids == 0)[:, None, None], env[None], 0.0)
    parent_mine = lookup(parent, node_ids)
    is_left = lookup(left, parent_mine) == node_ids
    onehot_parent = (parent_mine[:, None] == slots[None, :]).astype(jnp.float32)
    for level in range(LEVELS - 1):

        def descend(items, level=level):
            right_part, left_part, down_now, node_level = items

            def descend_compute(unused):
                moved_r = jnp.einsum("pq,rql->rpl", down_now, right_part, precision=HIGH)
                down_left = jnp.einsum("rpl,rpm->lm", right_part, moved_r, precision=HIGH)
                moved_l = jnp.einsum("pq,qlr->plr", down_now, left_part, precision=HIGH)
                down_right = jnp.einsum("plr,pls->rs", left_part, moved_l, precision=HIGH)
                return (down_left, down_right)

            def descend_keep(unused):
                return (zero_square, zero_square)

            return lax.cond(node_level == level, descend_compute, descend_keep, 0)

        part_left, part_right = lax.map(descend, (right_form, left_form, down, my_level))
        rows_left, rows_right = (
            lax.psum_scatter(part_left, "slab", scatter_dimension=1, tiled=True),
            lax.psum_scatter(part_right, "slab", scatter_dimension=1, tiled=True),
        )
        every_left, every_right = (
            lax.all_gather(rows_left, "node", axis=0, tiled=True),
            lax.all_gather(rows_right, "node", axis=0, tiled=True),
        )
        from_left = select_rows(onehot_parent, every_left)
        from_right = select_rows(onehot_parent, every_right)
        mine = jnp.where(is_left[:, None, None], from_left, from_right)
        full_down = lax.all_gather(mine, "slab", axis=1, tiled=True)
        down = jnp.where((my_level == level + 1)[:, None, None], full_down, down)
    factor = width**0.75
    own_part = jnp.einsum("npq,nqlr->nplr", down, right_store, precision=HIGH)
    far_part = jnp.einsum("npq,nrql->nrpl", down, left_store, precision=HIGH)
    far_moved = lax.all_to_all(far_part, "slab", split_axis=3, concat_axis=1, tiled=True).transpose(
        0, 2, 3, 1
    )
    gradient = factor * (own_part + far_moved)
    return (gradient, energy)


def solution(mesh):
    return jax.shard_map(
        per_device,
        mesh=mesh,
        in_specs=(P("node", "slab", None, None), P(), P(), P(), P()),
        out_specs=(P("node", None, "slab", None), P()),
        check_vma=False,
    )
```

profile of v0, /device:TPU:1, one launch (start us, length us, event | category | flops | bytes accessed | tf_op | source)
XLA Modules:
  0.0 1453.6 jit_solution(2452833348320943357)
XLA Ops:
  21.7 8.7 all-to-all-done.2
  36.1 8.7 all-to-all-done
  67.8 108.2 %all-reduce.23.cloned.1.call-done = f32[1,128,128]{2,1,0:T(8,128)} async-done(((f32[1,128,128]{2,1,0:T(8,128)}), f32[1,128,128]{2,1,0:T(8,128)}) %all-reduce.23.cloned.1.call-update) | async-done | bytes 65552
  176.7 37.1 %all_gather.84 = f32[16,8,128]{2,1,0:T(8,128)S(1)} all-gather(f32[1,8,128]{2,1,0:T(8,128)S(1)} %constant_dynamic-slice_fusion.3), channel_id=1, replica_groups=mesh['node'=16,'slab'=16] {'node'}, dimensions={0}, use_global_device_ids=true | all-gather | bytes 69632 | tf_op jit(solution)/shard_map/all_gather | solution.py:101
  215.3 25.6 %all-gather.5 = f32[128,128]{1,0:T(8,128)S(1)} all-gather(f32[8,128]{1,0:T(8,128)S(1)} %bitcast.485), channel_id=7, replica_groups=mesh['node'=16,'slab'=16] {'slab'}, dimensions={0}, use_global_device_ids=true | all-gather | bytes 69632 | tf_op jit(solution)/shard_map/all_gather | solution.py:106
  240.9 18.1 %all-gather.4 = f32[128,128]{1,0:T(8,128)S(1)} all-gather(f32[8,128]{1,0:T(8,128)S(1)} %bitcast.484), channel_id=6, replica_groups=mesh['node'=16,'slab'=16] {'slab'}, dimensions={0}, use_global_device_ids=true | all-gather | bytes 69632 | tf_op jit(solution)/shard_map/all_gather | solution.py:105
  263.6 106.7 %all-reduce.31.cloned.1.call-done = (f32[1,128,128]{2,1,0:T(8,128)}, f32[1,128,128]{2,0,1:T(1,128)}, f32[1,128,128]{2,0,1:T(1,128)}) async-done(((f32[1,128,128]{2,1,0:T(8,128)}, f32[1,128,128]{2,0,1:T(1,128)}, f32[1,128,128]{2,0,1:T(1,128)}), (f32[1,128,128]{2,1,0:T(8,128)}, f32[1,128,128]{2,0,1:T(1,128)}, f32[1,128,128]{2,0,1:T(1,128)})) %all-reduce.31.cloned.1.call-update) | async-done | bytes 196624
  370.9 37.4 %all_gather.87 = f32[16,8,128]{2,1,0:T(8,128)S(1)} all-gather(f32[1,8,128]{2,1,0:T(8,128)S(1)} %constant_dynamic-slice_fusion.2), channel_id=1, replica_groups=mesh['node'=16,'slab'=16] {'node'}, dimensions={0}, use_global_device_ids=true | all-gather | bytes 69632 | tf_op jit(solution)/shard_map/all_gather | solution.py:101
  411.3 24.4 %all-gather.7 = f32[128,128]{1,0:T(8,128)S(1)} all-gather(f32[8,128]{1,0:T(8,128)S(1)} %bitcast.477), channel_id=9, replica_groups=mesh['node'=16,'slab'=16] {'slab'}, dimensions={0}, use_global_device_ids=true | all-gather | bytes 69632 | tf_op jit(solution)/shard_map/all_gather | solution.py:106
  435.7 18.1 %all-gather.6 = f32[128,128]{1,0:T(8,128)S(1)} all-gather(f32[8,128]{1,0:T(8,128)S(1)} %bitcast.475), channel_id=8, replica_groups=mesh['node'=16,'slab'=16] {'slab'}, dimensions={0}, use_global_device_ids=true | all-gather | bytes 69632 | tf_op jit(solution)/shard_map/all_gather | solution.py:105
  453.8 31.3 %all_gather.73 = f32[16,8,128]{2,1,0:T(8,128)S(1)} all-gather(f32[1,8,128]{2,1,0:T(8,128)S(1)} %bitcast.492), channel_id=1, replica_groups=mesh['node'=16,'slab'=16] {'node'}, dimensions={0}, use_global_device_ids=true | all-gather | bytes 69632 | tf_op jit(solution)/shard_map/all_gather | solution.py:145
  485.9 33.3 %all_gather.72 = f32[16,8,128]{2,1,0:T(8,128)S(1)} all-gather(f32[1,8,128]{2,1,0:T(8,128)S(1)} %bitcast.489), channel_id=1, replica_groups=mesh['node'=16,'slab'=16] {'node'}, dimensions={0}, use_global_device_ids=true | all-gather | bytes 69632 | tf_op jit(solution)/shard_map/all_gather | solution.py:144
  520.0 30.2 %all-gather = f32[128,128]{1,0:T(8,128)S(1)} all-gather(f32[8,128]{1,0:T(8,128)S(1)} %broadcast_select_fusion.4), channel_id=2, replica_groups=mesh['node'=16,'slab'=16] {'slab'}, dimensions={0}, use_global_device_ids=true | all-gather | bytes 69632 | tf_op jit(solution)/shard_map/all_gather | solution.py:150
  552.5 112.1 %all-reduce.29.cloned.1.call-done = (f32[1,128,128]{2,1,0:T(8,128)}, f32[1,128,128]{2,0,1:T(1,128)}, f32[1,128,128]{2,0,1:T(1,128)}) async-done(((f32[1,128,128]{2,1,0:T(8,128)}, f32[1,128,128]{2,0,1:T(1,128)}, f32[1,128,128]{2,0,1:T(1,128)}), (f32[1,128,128]{2,1,0:T(8,128)}, f32[1,128,128]{2,0,1:T(1,128)}, f32[1,128,128]{2,0,1:T(1,128)})) %all-reduce.29.cloned.1.call-update) | async-done | bytes 196624
  665.3 37.4 %all_gather.90 = f32[16,8,128]{2,1,0:T(8,128)S(1)} all-gather(f32[1,8,128]{2,1,0:T(8,128)S(1)} %constant_dynamic-slice_fusion.1), channel_id=1, replica_groups=mesh['node'=16,'slab'=16] {'node'}, dimensions={0}, use_global_device_ids=true | all-gather | bytes 69632 | tf_op jit(solution)/shard_map/all_gather | solution.py:101
  705.7 24.4 %all-gather.9 = f32[128,128]{1,0:T(8,128)S(1)} all-gather(f32[8,128]{1,0:T(8,128)S(1)} %bitcast.478), channel_id=11, replica_groups=mesh['node'=16,'slab'=16] {'slab'}, dimensions={0}, use_global_device_ids=true | all-gather | bytes 69632 | tf_op jit(solution)/shard_map/all_gather | solution.py:106
  730.0 18.1 %all-gather.8 = f32[128,128]{1,0:T(8,128)S(1)} all-gather(f32[8,128]{1,0:T(8,128)S(1)} %bitcast.476), channel_id=10, replica_groups=mesh['node'=16,'slab'=16] {'slab'}, dimensions={0}, use_global_device_ids=true | all-gather | bytes 69632 | tf_op jit(solution)/shard_map/all_gather | solution.py:105
  748.2 31.3 %all_gather.76 = f32[16,8,128]{2,1,0:T(8,128)S(1)} all-gather(f32[1,8,128]{2,1,0:T(8,128)S(1)} %bitcast.493), channel_id=1, replica_groups=mesh['node'=16,'slab'=16] {'node'}, dimensions={0}, use_global_device_ids=true | all-gather | bytes 69632 | tf_op jit(solution)/shard_map/all_gather | solution.py:145
  780.3 33.3 %all_gather.75 = f32[16,8,128]{2,1,0:T(8,128)S(1)} all-gather(f32[1,8,128]{2,1,0:T(8,128)S(1)} %bitcast.490), channel_id=1, replica_groups=mesh['node'=16,'slab'=16] {'node'}, dimensions={0}, use_global_device_ids=true | all-gather | bytes 69632 | tf_op jit(solution)/shard_map/all_gather | solution.py:144
  814.4 30.2 %all-gather.1 = f32[128,128]{1,0:T(8,128)S(1)} all-gather(f32[8,128]{1,0:T(8,128)S(1)} %broadcast_select_fusion.3), channel_id=3, replica_groups=mesh['node'=16,'slab'=16] {'slab'}, dimensions={0}, use_global_device_ids=true | all-gather | bytes 69632 | tf_op jit(solution)/shard_map/all_gather | solution.py:150
  847.0 113.2 %all-reduce.27.cloned.1.call-done = (f32[1,128,128]{2,1,0:T(8,128)}, f32[1,128,128]{2,0,1:T(1,128)}, f32[1,128,128]{2,0,1:T(1,128)}) async-done(((f32[1,128,128]{2,1,0:T(8,128)}, f32[1,128,128]{2,0,1:T(1,128)}, f32[1,128,128]{2,0,1:T(1,128)}), (f32[1,128,128]{2,1,0:T(8,128)}, f32[1,128,128]{2,0,1:T(1,128)}, f32[1,128,128]{2,0,1:T(1,128)})) %all-reduce.27.cloned.1.call-update) | async-done | bytes 196624
  960.9 37.4 %all_gather.93 = f32[16,8,128]{2,1,0:T(8,128)S(1)} all-gather(f32[1,8,128]{2,1,0:T(8,128)S(1)} %constant_dynamic-slice_fusion), channel_id=1, replica_groups=mesh['node'=16,'slab'=16] {'node'}, dimensions={0}, use_global_device_ids=true | all-gather | bytes 69632 | tf_op jit(solution)/shard_map/all_gather | solution.py:101
  1001.2 24.3 %all-gather.11 = f32[128,128]{1,0:T(8,128)S(1)} all-gather(f32[8,128]{1,0:T(8,128)S(1)} %bitcast.473), channel_id=13, replica_groups=mesh['node'=16,'slab'=16] {'slab'}, dimensions={0}, use_global_device_ids=true | all-gather | bytes 69632 | tf_op jit(solution)/shard_map/all_gather | solution.py:106
  1025.6 18.1 %all-gather.10 = f32[128,128]{1,0:T(8,128)S(1)} all-gather(f32[8,128]{1,0:T(8,128)S(1)} %bitcast.474), channel_id=12, replica_groups=mesh['node'=16,'slab'=16] {'slab'}, dimensions={0}, use_global_device_ids=true | all-gather | bytes 69632 | tf_op jit(solution)/shard_map/all_gather | solution.py:105
  1043.7 31.3 %all_gather.79 = f32[16,8,128]{2,1,0:T(8,128)S(1)} all-gather(f32[1,8,128]{2,1,0:T(8,128)S(1)} %bitcast.494), channel_id=1, replica_groups=mesh['node'=16,'slab'=16] {'node'}, dimensions={0}, use_global_device_ids=true | all-gather | bytes 69632 | tf_op jit(solution)/shard_map/all_gather | solution.py:145
  1075.8 33.3 %all_gather.78 = f32[16,8,128]{2,1,0:T(8,128)S(1)} all-gather(f32[1,8,128]{2,1,0:T(8,128)S(1)} %bitcast.491), channel_id=1, replica_groups=mesh['node'=16,'slab'=16] {'node'}, dimensions={0}, use_global_device_ids=true | all-gather | bytes 69632 | tf_op jit(solution)/shard_map/all_gather | solution.py:144
  1109.9 30.2 %all-gather.2 = f32[128,128]{1,0:T(8,128)S(1)} all-gather(f32[8,128]{1,0:T(8,128)S(1)} %broadcast_select_fusion.2), channel_id=4, replica_groups=mesh['node'=16,'slab'=16] {'slab'}, dimensions={0}, use_global_device_ids=true | all-gather | bytes 69632 | tf_op jit(solution)/shard_map/all_gather | solution.py:150
  1149.5 108.8 %all-reduce.25.cloned.1.call-done = (f32[1,128,128]{2,0,1:T(1,128)}, f32[1,128,128]{2,0,1:T(1,128)}, f32[1,128,128]{2,1,0:T(8,128)}) async-done(((f32[1,128,128]{2,0,1:T(1,128)}, f32[1,128,128]{2,0,1:T(1,128)}, f32[1,128,128]{2,1,0:T(8,128)}), (f32[1,128,128]{2,0,1:T(1,128)}, f32[1,128,128]{2,0,1:T(1,128)}, f32[1,128,128]{2,1,0:T(8,128)})) %all-reduce.25.cloned.1.call-update) | async-done | bytes 196624
  1259.6 37.4 %all_gather.81 = f32[16,8,128]{2,1,0:T(8,128)S(1)} all-gather(f32[1,8,128]{2,1,0:T(8,128)S(1)} %bitcast.496), channel_id=1, replica_groups=mesh['node'=16,'slab'=16] {'node'}, dimensions={0}, use_global_device_ids=true | all-gather | bytes 69632 | tf_op jit(solution)/shard_map/all_gather | solution.py:144
  1297.8 31.3 %all_gather.82 = f32[16,8,128]{2,1,0:T(8,128)S(1)} all-gather(f32[1,8,128]{2,1,0:T(8,128)S(1)} %bitcast.495), channel_id=1, replica_groups=mesh['node'=16,'slab'=16] {'node'}, dimensions={0}, use_global_device_ids=true | all-gather | bytes 69632 | tf_op jit(solution)/shard_map/all_gather | solution.py:145
  1329.9 31.3 %all-gather.3 = f32[128,128]{1,0:T(8,128)S(1)} all-gather(f32[8,128]{1,0:T(8,128)S(1)} %broadcast_select_fusion.1), channel_id=5, replica_groups=mesh['node'=16,'slab'=16] {'slab'}, dimensions={0}, use_global_device_ids=true | all-gather | bytes 69632 | tf_op jit(solution)/shard_map/all_gather | solution.py:150
  1369.4 75.3 %psum.7 = f32[]{:T(128)} all-reduce(f32[]{:T(128)S(6)} %select_n.174), channel_id=1, replica_groups=mesh['node'=16,'slab'=16] {'node','slab'}, use_global_device_ids=true, to_apply=%region_43.44 | all-reduce | flops 1 | bytes 8 | tf_op jit(solution)/shard_map/psum | solution.py:116
  (155 shorter events, 94.4 us)
Async XLA Ops:
  7.2 1.4 copy-start
  7.2 0.7 copy-start.15
  8.6 2.7 copy-start.6
  13.5 16.8 %all-to-all-start.2 = ((f32[1,8,128,128]{3,1,0,2:T(8,128)}), f32[1,8,128,128]{3,1,0,2:T(8,128)S(1)}, u32[]{:S(2)}, u32[]{:S(2)}) async-start(f32[1,8,128,128]{3,1,0,2:T(8,128)} %copy.218), calls=%async_computation.2 | async-start | bytes 1048576 | tf_op jit(solution)/shard_map/all_to_all | solution.py:55
  30.4 14.4 all-to-all-start
  44.7 7.4 copy-start.16
  44.7 10.2 copy-start.17
  44.8 14.5 all-to-all-start.1
  49.5 7.3 copy-start.9
  49.5 126.5 %all-reduce.23.cloned.1.call-start = ((), (), s32[]{:S(2)}) async-start(), calls=%async_computation.4 | async-start | bytes 131072
  61.0 0.6 copy-start.14
  61.7 308.6 %all-reduce.31.cloned.1.call-start = ((), (), s32[]{:S(2)}) async-start(), calls=%async_computation.8 | async-start | bytes 393216
  259.6 0.6 copy-start.11
  260.3 404.3 %all-reduce.29.cloned.1.call-start = ((), (), s32[]{:S(2)}) async-start(), calls=%async_computation.7 | async-start | bytes 393216
  551.8 0.6 copy-start.12
  552.4 407.7 %all-reduce.27.cloned.1.call-start = ((), (), s32[]{:S(2)}) async-start(), calls=%async_computation.6 | async-start | bytes 393216
  846.3 0.6 copy-start.13
  847.0 411.3 %all-reduce.25.cloned.1.call-start = ((), (), s32[]{:S(2)}) async-start(), calls=%async_computation.5 | async-start | bytes 393216
  1140.1 1.5 copy-start.5
  1143.5 1.0 copy-start.7
  1146.1 2.1 copy-start.8
  1148.2 0.6 copy-start.10
  1364.0 80.8 %all-to-all-start.3 = ((f32[1,8,128,128]{2,1,0,3:T(8,128)}), f32[1,8,128,128]{2,1,0,3:T(8,128)S(1)}, u32[]{:S(2)}, u32[]{:S(2)}) async-start(f32[1,8,128,128]{2,1,0,3:T(8,128)} %copy.233), calls=%async_computation.3 | async-start | bytes 1048576 | tf_op jit(solution)/shard_map/all_to_all | solution.py:155
Sparse Core Ops, SparseCore 0:
  61.8 114.1 all-reduce.22
  260.4 109.8 all-reduce.30
  552.6 111.9 all-reduce.28
  847.1 113.0 all-reduce.26
  1149.0 109.2 all-reduce.24
where the time goes:
time: 1460 us; the launch traced here: 1450 us
  blocking collectives  780 us (53%)
  waiting for transfers between devices  569 us (39%)
  matrix products  27.1 us (2%)
  local copies, waits for them, and re-layouts  26.8 us (2%)
  between operations  23.6 us (2%)
  starting transfers between devices  20.3 us (1%)
    unnamed x10, waiting for transfers between devices  549 us
    all_gather x4, blocking collectives, per_device(): every_rows = lax.all_gather(up_rows, 'node', axis=0, tiled=True)  149 us
    all_gather x4, blocking collectives, per_device(): lax.all_gather(rows_left, 'node', axis=0, tiled=True)  137 us
    all_gather x4, blocking collectives, per_device(): lax.all_gather(rows_right, 'node', axis=0, tiled=True)  125 us
    all_gather x4, blocking collectives, per_device(): full_down = lax.all_gather(mine, 'slab', axis=1, tiled=True)  122 us
    all_gather x4, blocking collectives, per_device(): lax.all_gather(right_rows, 'slab', axis=1, tiled=True)  98.7 us
    psum x1, blocking collectives, per_device(): energy = lax.psum(jnp.sum(own), ('node', 'slab'))  75.3 us
    all_gather x4, blocking collectives, per_device(): lax.all_gather(left_rows, 'slab', axis=1, tiled=True)  72.6 us
  transfers between devices with their start and end apart: 9, of which 8 were waited for; matrix products, arithmetic and copies ran while one was open for 1% of the time, Pallas kernels for 0%

commit v1 on v0

--- a/solution.py
+++ b/solution.py
@@ -6,6 +6,11 @@
 LEVELS = 5
 NODES = 16
 HIGH = lax.Precision.HIGHEST
+
+
+def swapped_in(x, axis, dim):
+    stack = jnp.stack([x] * lax.axis_size(axis))
+    return jnp.concatenate(lax.all_to_all(stack, axis, 0, 0), axis=dim)
 
 
 def links(parent):
@@ -141,7 +146,7 @@
             lax.psum_scatter(part_right, "slab", scatter_dimension=1, tiled=True),
         )
         every_left, every_right = (
-            lax.all_gather(rows_left, "node", axis=0, tiled=True),
+            swapped_in(rows_left, "node", 0),
             lax.all_gather(rows_right, "node", axis=0, tiled=True),
         )
         from_left = select_rows(onehot_parent, every_left)

time: 1460 us -> 1350 us (0.925)
  blocking collectives: 780 us -> 625 us
  waiting for transfers between devices: 569 us -> 592 us
  starting transfers between devices: 20.3 us -> 42.1 us
    all_gather x4 -> x0, blocking collectives: 137 us -> none  [per_device(): lax.all_gather(rows_left, 'node', axis=0, tiled=True)]
    all_gather x4, blocking collectives: 122 us -> 99.7 us  [per_device(): full_down = lax.all_gather(mine, 'slab', axis=1, tiled=True)]
    all_to_all x0 -> x4, starting transfers between devices: none -> 21.8 us  [swapped_in(): return jnp.concatenate(lax.all_to_all(stack, axis, 0, 0), axis=dim)]
    all_to_all x0 -> x4, waiting for transfers between devices: none -> 17.5 us  [swapped_in(): return jnp.concatenate(lax.all_to_all(stack, axis, 0, 0), axis=dim)]
  transfers between devices with their start and end apart: 9 -> 13, of which waited for: 8 -> 11; matrix products, arithmetic and copies ran while one was open for 1% -> 2% of each run, Pallas kernels for 0% -> 0%
where the time goes in v1:
time: 1350 us; the launch traced here: 1340 us
  blocking collectives  625 us (46%)
  waiting for transfers between devices  592 us (44%)
  starting transfers between devices  42.1 us (3%)
  local copies, waits for them, and re-layouts  27.5 us (2%)
  matrix products  26.6 us (2%)
  between operations  23.6 us (2%)
    unnamed x10, waiting for transfers between devices  555 us
    all_gather x4, blocking collectives, per_device(): every_rows = lax.all_gather(up_rows, 'node', axis=0, tiled=True)  149 us
    all_gather x4, blocking collectives, per_device(): lax.all_gather(rows_right, 'node', axis=0, tiled=True)  131 us
    all_gather x4, blocking collectives, per_device(): full_down = lax.all_gather(mine, 'slab', axis=1, tiled=True)  99.7 us
    all_gather x4, blocking collectives, per_device(): lax.all_gather(right_rows, 'slab', axis=1, tiled=True)  98.6 us
    psum x1, blocking collectives, per_device(): energy = lax.psum(jnp.sum(own), ('node', 'slab'))  74.1 us
    all_gather x4, blocking collectives, per_device(): lax.all_gather(left_rows, 'slab', axis=1, tiled=True)  72.6 us
  transfers between devices with their start and end apart: 13, of which 11 were waited for; matrix products, arithmetic and copies ran while one was open for 2% of the time, Pallas kernels for 0%

profile of v1, /device:TPU:1, one launch (start us, length us, event | category | flops | bytes accessed | tf_op | source)
XLA Modules:
  0.0 1344.1 jit_solution(9218602184468659610)
XLA Ops:
  13.6 7.2 all-to-all-start.6
  21.7 8.7 all-to-all-done.6
  36.1 8.6 all-to-all-done
  67.8 108.3 %all-reduce.23.cloned.1.call-done = f32[1,128,128]{2,1,0:T(8,128)} async-done(((f32[1,128,128]{2,1,0:T(8,128)}), f32[1,128,128]{2,1,0:T(8,128)}) %all-reduce.23.cloned.1.call-update) | async-done | bytes 65552
  176.9 37.1 %all_gather.68 = f32[16,8,128]{2,1,0:T(8,128)S(1)} all-gather(f32[1,8,128]{2,1,0:T(8,128)S(1)} %constant_dynamic-slice_fusion.3), channel_id=1, replica_groups=mesh['node'=16,'slab'=16] {'node'}, dimensions={0}, use_global_device_ids=true | all-gather | bytes 69632 | tf_op jit(solution)/shard_map/all_gather | solution.py:106
  215.4 25.6 %all-gather.5 = f32[128,128]{1,0:T(8,128)S(1)} all-gather(f32[8,128]{1,0:T(8,128)S(1)} %bitcast.495), channel_id=7, replica_groups=mesh['node'=16,'slab'=16] {'slab'}, dimensions={0}, use_global_device_ids=true | all-gather | bytes 69632 | tf_op jit(solution)/shard_map/all_gather | solution.py:111
  241.0 18.1 %all-gather.4 = f32[128,128]{1,0:T(8,128)S(1)} all-gather(f32[8,128]{1,0:T(8,128)S(1)} %bitcast.494), channel_id=6, replica_groups=mesh['node'=16,'slab'=16] {'slab'}, dimensions={0}, use_global_device_ids=true | all-gather | bytes 69632 | tf_op jit(solution)/shard_map/all_gather | solution.py:110
  263.6 106.8 %all-reduce.31.cloned.1.call-done = (f32[1,128,128]{2,1,0:T(8,128)}, f32[1,128,128]{2,0,1:T(1,128)}, f32[1,128,128]{2,0,1:T(1,128)}) async-done(((f32[1,128,128]{2,1,0:T(8,128)}, f32[1,128,128]{2,0,1:T(1,128)}, f32[1,128,128]{2,0,1:T(1,128)}), (f32[1,128,128]{2,1,0:T(8,128)}, f32[1,128,128]{2,0,1:T(1,128)}, f32[1,128,128]{2,0,1:T(1,128)})) %all-reduce.31.cloned.1.call-update) | async-done | bytes 196624
  371.0 37.4 %all_gather.71 = f32[16,8,128]{2,1,0:T(8,128)S(1)} all-gather(f32[1,8,128]{2,1,0:T(8,128)S(1)} %constant_dynamic-slice_fusion.2), channel_id=1, replica_groups=mesh['node'=16,'slab'=16] {'node'}, dimensions={0}, use_global_device_ids=true | all-gather | bytes 69632 | tf_op jit(solution)/shard_map/all_gather | solution.py:106
  411.2 24.3 %all-gather.7 = f32[128,128]{1,0:T(8,128)S(1)} all-gather(f32[8,128]{1,0:T(8,128)S(1)} %bitcast.491), channel_id=9, replica_groups=mesh['node'=16,'slab'=16] {'slab'}, dimensions={0}, use_global_device_ids=true | all-gather | bytes 69632 | tf_op jit(solution)/shard_map/all_gather | solution.py:111
  435.6 18.1 %all-gather.6 = f32[128,128]{1,0:T(8,128)S(1)} all-gather(f32[8,128]{1,0:T(8,128)S(1)} %bitcast.486), channel_id=8, replica_groups=mesh['node'=16,'slab'=16] {'slab'}, dimensions={0}, use_global_device_ids=true | all-gather | bytes 69632 | tf_op jit(solution)/shard_map/all_gather | solution.py:110
  453.7 31.3 %all_gather.60 = f32[16,8,128]{2,1,0:T(8,128)S(1)} all-gather(f32[1,8,128]{2,1,0:T(8,128)S(1)} %bitcast.503), channel_id=1, replica_groups=mesh['node'=16,'slab'=16] {'node'}, dimensions={0}, use_global_device_ids=true | all-gather | bytes 69632 | tf_op jit(solution)/shard_map/all_gather | solution.py:150
  490.8 8.0 all-to-all-done.2
  499.7 24.9 %all-gather = f32[128,128]{1,0:T(8,128)S(1)} all-gather(f32[8,128]{1,0:T(8,128)S(1)} %broadcast_select_fusion.4), channel_id=2, replica_groups=mesh['node'=16,'slab'=16] {'slab'}, dimensions={0}, use_global_device_ids=true | all-gather | bytes 69632 | tf_op jit(solution)/shard_map/all_gather | solution.py:155
  526.1 112.9 %all-reduce.29.cloned.1.call-done = (f32[1,128,128]{2,1,0:T(8,128)}, f32[1,128,128]{2,0,1:T(1,128)}, f32[1,128,128]{2,0,1:T(1,128)}) async-done(((f32[1,128,128]{2,1,0:T(8,128)}, f32[1,128,128]{2,0,1:T(1,128)}, f32[1,128,128]{2,0,1:T(1,128)}), (f32[1,128,128]{2,1,0:T(8,128)}, f32[1,128,128]{2,0,1:T(1,128)}, f32[1,128,128]{2,0,1:T(1,128)})) %all-reduce.29.cloned.1.call-update) | async-done | bytes 196624
  639.6 37.4 %all_gather.74 = f32[16,8,128]{2,1,0:T(8,128)S(1)} all-gather(f32[1,8,128]{2,1,0:T(8,128)S(1)} %constant_dynamic-slice_fusion.1), channel_id=1, replica_groups=mesh['node'=16,'slab'=16] {'node'}, dimensions={0}, use_global_device_ids=true | all-gather | bytes 69632 | tf_op jit(solution)/shard_map/all_gather | solution.py:106
  679.9 24.3 %all-gather.9 = f32[128,128]{1,0:T(8,128)S(1)} all-gather(f32[8,128]{1,0:T(8,128)S(1)} %bitcast.492), channel_id=11, replica_groups=mesh['node'=16,'slab'=16] {'slab'}, dimensions={0}, use_global_device_ids=true | all-gather | bytes 69632 | tf_op jit(solution)/shard_map/all_gather | solution.py:111
  704.2 18.1 %all-gather.8 = f32[128,128]{1,0:T(8,128)S(1)} all-gather(f32[8,128]{1,0:T(8,128)S(1)} %bitcast.488), channel_id=10, replica_groups=mesh['node'=16,'slab'=16] {'slab'}, dimensions={0}, use_global_device_ids=true | all-gather | bytes 69632 | tf_op jit(solution)/shard_map/all_gather | solution.py:110
  722.3 31.3 %all_gather.62 = f32[16,8,128]{2,1,0:T(8,128)S(1)} all-gather(f32[1,8,128]{2,1,0:T(8,128)S(1)} %bitcast.504), channel_id=1, replica_groups=mesh['node'=16,'slab'=16] {'node'}, dimensions={0}, use_global_device_ids=true | all-gather | bytes 69632 | tf_op jit(solution)/shard_map/all_gather | solution.py:150
  759.7 7.8 all-to-all-done.3
  768.3 24.9 %all-gather.1 = f32[128,128]{1,0:T(8,128)S(1)} all-gather(f32[8,128]{1,0:T(8,128)S(1)} %broadcast_select_fusion.3), channel_id=3, replica_groups=mesh['node'=16,'slab'=16] {'slab'}, dimensions={0}, use_global_device_ids=true | all-gather | bytes 69632 | tf_op jit(solution)/shard_map/all_gather | solution.py:155
  794.7 113.8 %all-reduce.27.cloned.1.call-done = (f32[1,128,128]{2,1,0:T(8,128)}, f32[1,128,128]{2,0,1:T(1,128)}, f32[1,128,128]{2,0,1:T(1,128)}) async-done(((f32[1,128,128]{2,1,0:T(8,128)}, f32[1,128,128]{2,0,1:T(1,128)}, f32[1,128,128]{2,0,1:T(1,128)}), (f32[1,128,128]{2,1,0:T(8,128)}, f32[1,128,128]{2,0,1:T(1,128)}, f32[1,128,128]{2,0,1:T(1,128)})) %all-reduce.27.cloned.1.call-update) | async-done | bytes 196624
  909.2 37.4 %all_gather.77 = f32[16,8,128]{2,1,0:T(8,128)S(1)} all-gather(f32[1,8,128]{2,1,0:T(8,128)S(1)} %constant_dynamic-slice_fusion), channel_id=1, replica_groups=mesh['node'=16,'slab'=16] {'node'}, dimensions={0}, use_global_device_ids=true | all-gather | bytes 69632 | tf_op jit(solution)/shard_map/all_gather | solution.py:106
  949.4 24.3 %all-gather.11 = f32[128,128]{1,0:T(8,128)S(1)} all-gather(f32[8,128]{1,0:T(8,128)S(1)} %bitcast.484), channel_id=13, replica_groups=mesh['node'=16,'slab'=16] {'slab'}, dimensions={0}, use_global_device_ids=true | all-gather | bytes 69632 | tf_op jit(solution)/shard_map/all_gather | solution.py:111
  973.8 18.1 %all-gather.10 = f32[128,128]{1,0:T(8,128)S(1)} all-gather(f32[8,128]{1,0:T(8,128)S(1)} %bitcast.485), channel_id=12, replica_groups=mesh['node'=16,'slab'=16] {'slab'}, dimensions={0}, use_global_device_ids=true | all-gather | bytes 69632 | tf_op jit(solution)/shard_map/all_gather | solution.py:110
  991.9 31.3 %all_gather.64 = f32[16,8,128]{2,1,0:T(8,128)S(1)} all-gather(f32[1,8,128]{2,1,0:T(8,128)S(1)} %bitcast.505), channel_id=1, replica_groups=mesh['node'=16,'slab'=16] {'node'}, dimensions={0}, use_global_device_ids=true | all-gather | bytes 69632 | tf_op jit(solution)/shard_map/all_gather | solution.py:150
  1037.9 24.9 %all-gather.2 = f32[128,128]{1,0:T(8,128)S(1)} all-gather(f32[8,128]{1,0:T(8,128)S(1)} %broadcast_select_fusion.2), channel_id=4, replica_groups=mesh['node'=16,'slab'=16] {'slab'}, dimensions={0}, use_global_device_ids=true | all-gather | bytes 69632 | tf_op jit(solution)/shard_map/all_gather | solution.py:155
  1065.1 113.1 %all-reduce.25.cloned.1.call-done = (f32[1,128,128]{2,0,1:T(1,128)}, f32[1,128,128]{2,0,1:T(1,128)}, f32[1,128,128]{2,1,0:T(8,128)}) async-done(((f32[1,128,128]{2,0,1:T(1,128)}, f32[1,128,128]{2,0,1:T(1,128)}, f32[1,128,128]{2,1,0:T(8,128)}), (f32[1,128,128]{2,0,1:T(1,128)}, f32[1,128,128]{2,0,1:T(1,128)}, f32[1,128,128]{2,1,0:T(8,128)})) %all-reduce.25.cloned.1.call-update) | async-done | bytes 196624
  1180.2 9.0 all-to-all-start.5
  1189.2 36.9 %all_gather.66 = f32[16,8,128]{2,1,0:T(8,128)S(1)} all-gather(f32[1,8,128]{2,1,0:T(8,128)S(1)} %bitcast.502), channel_id=1, replica_groups=mesh['node'=16,'slab'=16] {'node'}, dimensions={0}, use_global_device_ids=true | all-gather | bytes 69632 | tf_op jit(solution)/shard_map/all_gather | solution.py:150
  1227.8 25.1 %all-gather.3 = f32[128,128]{1,0:T(8,128)S(1)} all-gather(f32[8,128]{1,0:T(8,128)S(1)} %broadcast_select_fusion.1), channel_id=5, replica_groups=mesh['node'=16,'slab'=16] {'slab'}, dimensions={0}, use_global_device_ids=true | all-gather | bytes 69632 | tf_op jit(solution)/shard_map/all_gather | solution.py:155
  1261.1 74.1 %psum.7 = f32[]{:T(128)} all-reduce(f32[]{:T(128)S(6)} %select_n.174), channel_id=1, replica_groups=mesh['node'=16,'slab'=16] {'node','slab'}, use_global_device_ids=true, to_apply=%region_43.44 | all-reduce | flops 1 | bytes 8 | tf_op jit(solution)/shard_map/psum | solution.py:121
  (163 shorter events, 101.9 us)
Async XLA Ops:
  7.2 1.4 copy-start
  7.2 0.7 copy-start.15
  8.6 2.7 copy-start.6
  13.6 16.8 %all-to-all-start.6 = ((f32[1,8,128,128]{3,1,0,2:T(8,128)}), f32[1,8,128,128]{3,1,0,2:T(8,128)S(1)}, u32[]{:S(2)}, u32[]{:S(2)}) async-start(f32[1,8,128,128]{3,1,0,2:T(8,128)} %copy.218), calls=%async_computation.6 | async-start | bytes 1048576 | tf_op jit(solution)/shard_map/all_to_all | solution.py:60
  30.4 14.4 %all-to-all-start = ((f32[1,128,8,128]{3,2,0,1:T(8,128)}), f32[1,128,8,128]{3,2,0,1:T(8,128)S(1)}, u32[]{:S(2)}, u32[]{:S(2)}) async-start(f32[1,128,8,128]{3,2,0,1:T(8,128)} %bitcast.69), calls=%async_computation | async-start | bytes 1048576 | tf_op jit(solution)/shard_map/all_to_all | solution.py:55
  44.8 7.4 copy-start.16
  44.8 10.2 copy-start.17
  44.8 14.5 %all-to-all-start.1 = ((f32[1,8,128,128]{3,1,0,2:T(8,128)}), f32[1,8,128,128]{3,1,0,2:T(8,128)S(1)}, u32[]{:S(2)}, u32[]{:S(2)}) async-start(f32[1,8,128,128]{3,1,0,2:T(8,128)} %copy.203), calls=%async_computation.1 | async-start | bytes 1048576 | tf_op jit(solution)/shard_map/all_to_all | solution.py:59
  49.5 7.4 copy-start.9
  49.5 126.7 %all-reduce.23.cloned.1.call-start = ((), (), s32[]{:S(2)}) async-start(), calls=%async_computation.8 | async-start | bytes 131072
  61.0 0.6 copy-start.14
  61.7 308.7 %all-reduce.31.cloned.1.call-start = ((), (), s32[]{:S(2)}) async-start(), calls=%async_computation.12 | async-start | bytes 393216
  259.7 0.6 copy-start.11
  485.7 13.2 all-to-all-start.2
  489.9 149.0 %all-reduce.29.cloned.1.call-start = ((), (), s32[]{:S(2)}) async-start(), calls=%async_computation.11 | async-start | bytes 393216
  490.1 9.6 copy-start.12
  754.3 13.2 all-to-all-start.3
  758.6 150.0 %all-reduce.27.cloned.1.call-start = ((), (), s32[]{:S(2)}) async-start(), calls=%async_computation.10 | async-start | bytes 393216
  758.9 9.4 copy-start.13
  794.0 234.2 %copy-start.5 = (f32[128,8,128]{2,0,1:T(8,128)S(1)}, f32[128,8,128]{2,0,1:T(8,128)}, u32[]{:S(2)}) copy-start(f32[128,8,128]{2,0,1:T(8,128)} %get-tuple-element.477) | copy-start | bytes 1572868
  1023.9 13.2 all-to-all-start.4
  1028.1 150.1 %all-reduce.25.cloned.1.call-start = ((), (), s32[]{:S(2)}) async-start(), calls=%async_computation.9 | async-start | bytes 393216
  1029.9 1.0 copy-start.7
  1032.5 2.1 copy-start.8
  1034.6 3.2 copy-start.10
  1180.2 46.7 %all-to-all-start.5 = ((f32[16,1,8,128]{3,2,1,0:T(8,128)}), f32[16,1,8,128]{3,2,1,0:T(8,128)S(1)}, u32[]{:S(2)}, u32[]{:S(2)}) async-start(f32[16,1,8,128]{3,2,1,0:T(8,128)} %stack.11), calls=%async_computation.5 | async-start | bytes 131072 | tf_op jit(solution)/shard_map/all_to_all | solution.py:13
  1255.6 79.6 %all-to-all-start.7 = ((f32[1,8,128,128]{2,1,0,3:T(8,128)}), f32[1,8,128,128]{2,1,0,3:T(8,128)S(1)}, u32[]{:S(2)}, u32[]{:S(2)}) async-start(f32[1,8,128,128]{2,1,0,3:T(8,128)} %copy.233), calls=%async_computation.7 | async-start | bytes 1048576 | tf_op jit(solution)/shard_map/all_to_all | solution.py:160
Sparse Core Ops, SparseCore 0:
  61.8 114.3 all-reduce.22
  260.5 109.8 all-reduce.30
  526.2 112.7 all-reduce.28
  794.8 113.6 all-reduce.26
  1064.6 113.5 all-reduce.24
